TPU v7x, 256 devices: a whole 4x4x8 slice. The times are simulated.
256 devices in a mesh: mic: 4 (over y), seq: 64 (over z, x, core).
Axes of the slice: x: 4, y: 4, z: 8, core: 2. Of those that a mesh axis runs over, the one named last changes fastest.
Arguments:
- frames_in: bfloat16 [8, 32768, 512], P('mic', 'seq'), may hold values from -16 to 16
- w_qkv: bfloat16 [8, 512, 1536], P('mic'), may hold values from -0.25 to 0.25
- w_join: bfloat16 [4096, 1024], P(('mic', 'seq')), may hold values from -0.09375 to 0.09375
- norm_gain: float32 [1024], replicated, may hold values from 0.5 to 2
- w_router: bfloat16 [1024, 64], replicated, may hold values from -0.1875 to 0.1875
- w_gate: bfloat16 [64, 1024, 4096], P('seq', None, 'mic'), may hold values from -0.1875 to 0.1875
- w_up: bfloat16 [64, 1024, 4096], P('seq', None, 'mic'), may hold values from -0.1875 to 0.1875
- w_down: bfloat16 [64, 4096, 1024], P('seq', 'mic'), may hold values from -0.09375 to 0.09375
- expert_ids: int32 [64, 4, 128, 2], P('seq', 'mic'), may hold values from 0 to 63, all different within a row; in each aligned block of 128 rows (0 to 127, 128 to 255, ..., all dimensions but the last counted through in order) at most 6 rows name the same one
Outputs:
- layer_out: bfloat16 [64, 4, 128, 1024], P('seq', 'mic')
Inputs may be any that keep to these rules, and one draw needn't show every extreme that they name: `expert_ids`: in the rows of one block (128 frames) no expert is named more than 6 times, a bound that some block reaches; the two ids of a frame differ.
All inputs are finite; a program needn't handle non-finite values.
Results may differ from a plain program's by a relative error of at most 0.017.
Values may be sent and summed in bfloat16 or wider, within the bound.
A program may use at most 128 MiB of HBM per device.

v0:
```python
import jax
import jax.numpy as jnp
from jax import lax
from jax.sharding import PartitionSpec as P

MICS = 8
HEADS = 8
TOP = 2


def body(frames_in, w_qkv, w_join, norm_gain, w_router, w_gate, w_up, w_down, expert_ids):
    mic_count = lax.axis_size("mic")
    seq_count = lax.axis_size("seq")
    mic_local, span, chan_width = frames_in.shape
    frame_rows = span // mic_count
    head_dim = chan_width // HEADS
    model_width = w_join.shape[1]
    expert_count = w_router.shape[1]
    exp_local = w_gate.shape[0]
    capacity = max(2, 3 * TOP * frame_rows // (2 * expert_count))
    projected = jnp.einsum(
        "mfc,mce->mfe", frames_in, w_qkv, preferred_element_type=jnp.float32
    ).astype(jnp.bfloat16)
    projected = projected.reshape(mic_local, mic_count, frame_rows, 3 * chan_width)
    arrived_block = lax.all_to_all(projected, "mic", split_axis=1, concat_axis=0, tiled=True)
    arrived_block = arrived_block[:, 0]
    frame_count = arrived_block.shape[1]
    queries = arrived_block[..., :chan_width].reshape(MICS, frame_count, HEADS, head_dim)
    keys_all = arrived_block[..., chan_width : 2 * chan_width].reshape(
        MICS, frame_count, HEADS, head_dim
    )
    values_all = arrived_block[..., 2 * chan_width :].reshape(MICS, frame_count, HEADS, head_dim)
    scores = jnp.einsum(
        "ifhd,jfhd->fhij", queries, keys_all, preferred_element_type=jnp.float32
    ) * head_dim ** (-0.5)
    row_max = jnp.max(scores, axis=-1, keepdims=True)
    weights = jnp.exp(scores - row_max)
    probs = (weights / jnp.sum(weights, axis=-1, keepdims=True)).astype(jnp.bfloat16)
    mixed_heads = jnp.einsum(
        "fhij,jfhd->fihd", probs, values_all, preferred_element_type=jnp.float32
    )
    attended = mixed_heads.astype(jnp.bfloat16).reshape(frame_count, MICS * chan_width)
    joined = jnp.dot(
        attended,
        lax.all_gather(w_join, ("mic", "seq"), axis=0, tiled=True),
        preferred_element_type=jnp.float32,
    )
    scale_row = lax.rsqrt(jnp.mean(joined * joined, axis=-1, keepdims=True) + 1e-06)
    normed = (joined * scale_row * norm_gain).astype(jnp.bfloat16)
    logits = jnp.dot(normed, w_router, preferred_element_type=jnp.float32)
    expert_rows = expert_ids.reshape(frame_rows, TOP)
    chosen = (expert_rows[..., None] == jnp.arange(expert_count, dtype=jnp.int32)).astype(jnp.int32)
    picked = jnp.sum(logits[:, None, :] * chosen.astype(jnp.float32), axis=-1)
    first_gate = 1.0 / (1.0 + jnp.exp(picked[:, 1] - picked[:, 0]))
    gates = jnp.stack([first_gate, 1.0 - first_gate], axis=-1)
    counts = jnp.sum(chosen, axis=1)
    before = jnp.cumsum(counts, axis=0) - counts
    slot_index = jnp.sum(before[:, None, :] * chosen, axis=-1)
    in_slot = slot_index[..., None] == jnp.arange(capacity, dtype=jnp.int32)
    mapped = (
        ((chosen[..., :, None] == 1) & in_slot[..., None, :])
        .reshape(frame_rows, TOP, expert_count * capacity)
        .astype(jnp.bfloat16)
    )
    merged_map = jnp.sum(mapped, axis=1)
    buffers = jnp.einsum(
        "rs,rd->sd", merged_map, normed, preferred_element_type=jnp.float32
    ).astype(jnp.bfloat16)
    buffers = buffers.reshape(seq_count, exp_local * capacity, model_width)
    landed = lax.all_to_all(buffers, "seq", split_axis=0, concat_axis=0, tiled=True)
    arrived = lax.all_gather(landed[None], "mic", axis=0, tiled=True)
    flat = arrived.reshape(mic_count * seq_count * exp_local * capacity, model_width)
    piece_rows = flat.reshape(-1, exp_local, capacity, model_width)
    first_proj = jnp.einsum(
        "nejd,edf->nejf", piece_rows, w_gate, preferred_element_type=jnp.float32
    )
    second_proj = jnp.einsum("nejd,edf->nejf", piece_rows, w_up, preferred_element_type=jnp.float32)
    inner = (jax.nn.silu(first_proj) * second_proj).astype(jnp.bfloat16)
    result = jnp.einsum("nejf,efd->nejd", inner, w_down, preferred_element_type=jnp.float32)
    summed = lax.psum_scatter(
        result.reshape(
            lax.axis_size("mic") * (seq_count * exp_local * capacity), model_width
        ).astype(jnp.bfloat16),
        "mic",
        scatter_dimension=0,
        tiled=True,
    ).astype(jnp.float32)
    summed = summed.astype(jnp.bfloat16).reshape(seq_count, exp_local * capacity, model_width)
    returned = lax.all_to_all(summed, "seq", split_axis=0, concat_axis=0, tiled=True)
    returned = returned.reshape(expert_count * capacity, model_width)
    picked_out = jnp.einsum("rks,sd->rkd", mapped, returned, preferred_element_type=jnp.float32)
    total = joined + jnp.sum(gates[..., None] * picked_out, axis=1)
    return total.astype(jnp.bfloat16).reshape(1, 1, frame_rows, model_width)


def solution(mesh):
    return jax.shard_map(
        body,
        mesh=mesh,
        in_specs=(
            P("mic", "seq", None),
            P("mic", None, None),
            P(("mic", "seq"), None),
            P(),
            P(),
            P("seq", None, "mic"),
            P("seq", None, "mic"),
            P("seq", "mic", None),
            P("seq", "mic", None, None),
        ),
        out_specs=P("seq", "mic", None, None),
        check_vma=False,
    )
```

profile of v0, /device:TPU:1, one launch (start us, length us, event | category | flops | bytes accessed | tf_op | source)
XLA Modules:
  0.0 346.4 jit_solution(7928431488291336185)
XLA Ops:
  8.4 3.0 convolution_convert_fusion
  11.5 2.0 copy.26
  13.4 5.1 %all-to-all-start = ((bf16[2,4,128,1536]{3,2,0,1:T(8,128)(2,1)}), bf16[2,4,128,1536]{3,2,0,1:T(8,128)(2,1)S(1)}, u32[]{:S(2)}, u32[]{:S(2)}) async-start(bf16[2,4,128,1536]{3,2,0,1:T(8,128)(2,1)} %copy.26), calls=%async_computation | async-start | bytes 6291456 | tf_op jit(solution)/shard_map/all_to_all | solution.py:25
  19.2 35.4 %all-to-all-done = bf16[2,4,128,1536]{3,2,0,1:T(8,128)(2,1)S(1)} async-done(((bf16[2,4,128,1536]{3,2,0,1:T(8,128)(2,1)}), bf16[2,4,128,1536]{3,2,0,1:T(8,128)(2,1)S(1)}, u32[]{:S(2)}, u32[]{:S(2)}) %all-to-all-start) | async-done | bytes 3145760 | tf_op jit(solution)/shard_map/all_to_all | solution.py:25
  58.1 3.8 %copy.30 = bf16[8,128,8,64]{3,0,2,1:T(8,128)(2,1)} copy(bf16[8,128,8,64]{1,3,2,0:T(8,128)(2,1)S(1)} %bitcast.103) | data formatting | bytes 2097152 | tf_op jit(solution)/shard_map/reshape | solution.py:28
  62.5 3.7 %copy.31 = bf16[8,128,8,64]{3,0,2,1:T(8,128)(2,1)} copy(bf16[8,128,8,64]{1,3,2,0:T(8,128)(2,1)S(1)} %bitcast.104) | data formatting | bytes 2097152 | tf_op jit(solution)/shard_map/reshape | solution.py:29
  66.9 3.7 %copy.32 = bf16[8,128,8,64]{3,0,2,1:T(8,128)(2,1)} copy(bf16[8,128,8,64]{1,3,2,0:T(8,128)(2,1)S(1)} %bitcast.105) | data formatting | bytes 2097152 | tf_op jit(solution)/shard_map/reshape | solution.py:32
  70.6 6.6 %fusion.38 = (f32[128,8,8]{2,1,0:T(8,128)S(1)}, f32[128,8,8,8]{2,3,1,0:T(8,128)}) fusion(bf16[8,128,8,64]{3,0,2,1:T(8,128)(2,1)S(1)} %copy-done.5, bf16[8,128,8,64]{3,0,2,1:T(8,128)(2,1)} %copy.31), kind=kOutput, calls=%fused_computation.56 | convolution fusion | flops 8585223 | bytes 2392064 | tf_op jit(solution)/shard_map/sub | solution.py:37
  77.2 4.7 %convert_bitcast_fusion.1 = bf16[128,8,8,64]{3,1,2,0:T(8,128)(2,1)} fusion(bf16[8,128,8,64]{3,0,2,1:T(8,128)(2,1)} %copy.32, f32[128,8,8,8]{2,3,1,0:T(8,128)} %get-tuple-element.11, f32[128,8,8]{2,1,0:T(8,128)S(1)} %get-tuple-element.10), kind=kOutput, calls=%fused_computation.22 | convolution fusion | flops 9043968 | bytes 2392064 | tf_op jit(solution)/shard_map/fhij,jfhd->fihd/dot_general | solution.py:39
  81.9 3.2 copy.34
  85.1 59.5 %all-gather.4.cloned.1.call-done = bf16[4096,1024]{1,0:T(8,128)(2,1)} async-done(((bf16[16,1024]{1,0:T(8,128)(2,1)}), bf16[4096,1024]{1,0:T(8,128)(2,1)}) %all-gather.4.cloned.1.call-update) | async-done | bytes 8388624 | tf_op jit(solution)/shard_map/all_gather | solution.py:45
  144.6 4.7 %multiply_reduce_fusion.1 = (f32[128]{0:T(128)S(1)}, f32[128,1024]{1,0:T(8,128)S(1)}) fusion(bf16[128,4096]{0,1:T(8,128)(2,1)S(1)} %bitcast.102, bf16[4096,1024]{1,0:T(8,128)(2,1)} %all-gather.4.cloned.1.call-done), kind=kOutput, calls=%fused_computation.33 | convolution fusion | flops 1074003840 | bytes 9961984 | tf_op jit(solution)/shard_map/dot_general | solution.py:43
  150.0 35.1 %all_to_all.25 = bf16[64,6,1024]{2,1,0:T(8,128)(2,1)S(1)} all-to-all(bf16[64,6,1024]{2,1,0:T(8,128)(2,1)S(1)} %reshape.92), channel_id=1, replica_groups=mesh['mic'=4,'seq'=64] {'seq'}, dimensions={0} | all-to-all | bytes 1572864 | tf_op jit(solution)/shard_map/all_to_all | solution.py:70
  186.5 37.7 %all-gather.6.cloned.1.call-done = bf16[256,6,1024]{2,0,1:T(8,128)(2,1)} async-done(((bf16[64,6,1024]{2,0,1:T(8,128)(2,1)}), bf16[256,6,1024]{2,0,1:T(8,128)(2,1)}) %all-gather.6.cloned.1.call-update) | async-done | bytes 3145744 | tf_op jit(solution)/shard_map/all_gather | solution.py:71
  224.2 8.6 %fusion.19 = f32[256,6,1024]{2,0,1:T(8,128)} fusion(bf16[256,6,1024]{2,0,1:T(8,128)(2,1)} %all-gather.6.cloned.1.call-done, bf16[1,1024,1024]{2,1,0:T(8,128)(2,1)} %param.14), kind=kOutput, calls=%fused_computation.20 | convolution fusion | flops 3221225472 | bytes 11534336 | tf_op jit(solution)/shard_map/nejd,edf->nejf/dot_general | solution.py:74
  232.8 10.6 %convert_bitcast_fusion = bf16[256,1,6,1024]{3,0,2,1:T(8,128)(2,1)S(1)} fusion(f32[256,6,1024]{2,0,1:T(8,128)} %fusion.19, bf16[256,6,1024]{2,0,1:T(8,128)(2,1)} %all-gather.6.cloned.1.call-done, bf16[1,1024,1024]{2,1,0:T(8,128)(2,1)} %param.16, bf16[1,1024,1024]{2,1,0:T(8,128)(2,1)} %param.15), kind=kOutput, calls=%fused_computation.15 | convolution fusion | flops 6453460992 | bytes 16777216 | tf_op jit(solution)/shard_map/nejf,efd->nejd/dot_general | solution.py:79
  243.4 3.7 %copy.40 = bf16[256,1,6,1024]{3,2,0,1:T(8,128)(2,1)} copy(bf16[256,1,6,1024]{3,0,2,1:T(8,128)(2,1)S(1)} %convert_bitcast_fusion) | data formatting | bytes 6291456 | tf_op jit(solution)/shard_map/convert_element_type | solution.py:83
  247.1 6.3 %convert_element_type.71 = bf16[1536,1024]{1,0:T(8,128)(2,1)} reshape(bf16[256,1,6,1024]{3,2,0,1:T(8,128)(2,1)} %copy.40) | data formatting | bytes 6291456 | tf_op jit(solution)/shard_map/convert_element_type | solution.py:83
  253.5 41.3 %reduce-scatter.2.cloned.1.call-done = bf16[384,1024]{1,0:T(8,128)(2,1)} async-done(((bf16[1536,1024]{1,0:T(8,128)(2,1)}), bf16[384,1024]{1,0:T(8,128)(2,1)}) %reduce-scatter.2.cloned.1.call-update) | async-done | bytes 786448 | tf_op jit(solution)/shard_map/reduce_scatter | solution.py:80
  294.7 2.3 reshape.98
  297.1 10.8 %all-to-all-start.2 = ((bf16[64,6,1024]{2,1,0:T(8,128)(2,1)}), bf16[64,6,1024]{2,1,0:T(8,128)(2,1)}, u32[]{:S(2)}, u32[]{:S(2)}) async-start(bf16[64,6,1024]{2,1,0:T(8,128)(2,1)} %reshape.98), calls=%async_computation.3 | async-start | bytes 2097152 | tf_op jit(solution)/shard_map/all_to_all | solution.py:89
  309.3 26.5 %all-to-all-done.2 = bf16[64,6,1024]{2,1,0:T(8,128)(2,1)} async-done(((bf16[64,6,1024]{2,1,0:T(8,128)(2,1)}), bf16[64,6,1024]{2,1,0:T(8,128)(2,1)}, u32[]{:S(2)}, u32[]{:S(2)}) %all-to-all-start.2) | async-done | bytes 786464 | tf_op jit(solution)/shard_map/all_to_all | solution.py:89
  335.8 2.3 fusion.24
  338.1 1.8 fusion.28
  (47 shorter events, 10.7 us)
Async XLA Ops:
  6.5 1.9 copy-start
  6.5 138.0 %all-gather.4.cloned.1.call-start = ((), (), s32[]{:S(2)}) async-start(), calls=%async_computation.4 | async-start | bytes 8421376 | tf_op jit(solution)/shard_map/all_gather | solution.py:45
  13.4 5.2 %copy-start.8 = (s32[1,1,128,2]{2,3,1,0:T(2,128)S(1)}, s32[1,1,128,2]{2,3,1,0:T(2,128)}, u32[]{:S(2)}) copy-start(s32[1,1,128,2]{2,3,1,0:T(2,128)} %param.17) | copy-start | bytes 3076
  13.4 41.2 %all-to-all-start = ((bf16[2,4,128,1536]{3,2,0,1:T(8,128)(2,1)}), bf16[2,4,128,1536]{3,2,0,1:T(8,128)(2,1)S(1)}, u32[]{:S(2)}, u32[]{:S(2)}) async-start(bf16[2,4,128,1536]{3,2,0,1:T(8,128)(2,1)} %copy.26), calls=%async_computation | async-start | bytes 6291456 | tf_op jit(solution)/shard_map/all_to_all | solution.py:25
  18.6 205.6 %all-gather.6.cloned.1.call-start = ((), (), s32[]{:S(2)}) async-start(), calls=%async_computation.6 | async-start | bytes 3932160 | tf_op jit(solution)/shard_map/all_gather | solution.py:71
  56.4 5.5 %copy-start.4 = (bf16[8,128,512]{2,1,0:T(8,128)(2,1)S(1)}, bf16[8,128,512]{2,1,0:T(8,128)(2,1)}, u32[]{:S(2)}) copy-start(bf16[8,128,512]{2,1,0:T(8,128)(2,1)} %get-tuple-element.7) | copy-start | bytes 3145732
  61.8 4.4 %copy-start.3 = (bf16[8,128,512]{2,1,0:T(8,128)(2,1)S(1)}, bf16[8,128,512]{2,1,0:T(8,128)(2,1)}, u32[]{:S(2)}) copy-start(bf16[8,128,512]{2,1,0:T(8,128)(2,1)} %get-tuple-element.9) | copy-start | bytes 3145732
  66.9 3.8 %copy-start.5 = (bf16[8,128,8,64]{3,0,2,1:T(8,128)(2,1)S(1)}, bf16[8,128,8,64]{3,0,2,1:T(8,128)(2,1)}, u32[]{:S(2)}) copy-start(bf16[8,128,8,64]{3,0,2,1:T(8,128)(2,1)} %copy.30) | copy-start | bytes 3145732
  144.6 4.8 %copy-start.7 = (f32[1024]{0:T(1024)S(1)}, f32[1024]{0:T(1024)}, u32[]{:S(2)}) copy-start(f32[1024]{0:T(1024)} %param.12) | copy-start | bytes 12292
  149.3 37.1 %copy-start.2 = (f32[128,1024]{1,0:T(8,128)}, f32[128,1024]{1,0:T(8,128)S(1)}, u32[]{:S(2)}) copy-start(f32[128,1024]{1,0:T(8,128)S(1)} %get-tuple-element.13) | copy-start | bytes 1572868
  186.5 108.3 %reduce-scatter.2.cloned.1.call-start = ((), (), s32[]{:S(2)}) async-start(), calls=%async_computation.5 | async-start | bytes 3932160 | tf_op jit(solution)/shard_map/reduce_scatter | solution.py:80
  253.4 54.4 %copy-start.6 = (bf16[1024,64]{0,1:T(8,128)(2,1)S(1)}, bf16[1024,64]{0,1:T(8,128)(2,1)}, u32[]{:S(2)}) copy-start(bf16[1024,64]{0,1:T(8,128)(2,1)} %param.13) | copy-start | bytes 393220
  294.7 45.2 %copy-start.1 = (bf16[2,512,1536]{2,1,0:T(8,128)(2,1)S(1)}, bf16[2,512,1536]{2,1,0:T(8,128)(2,1)}, u32[]{:S(2)}) copy-start(bf16[2,512,1536]{2,1,0:T(8,128)(2,1)} %param.10) | copy-start | bytes 9437188
  297.1 38.7 %all-to-all-start.2 = ((bf16[64,6,1024]{2,1,0:T(8,128)(2,1)}), bf16[64,6,1024]{2,1,0:T(8,128)(2,1)}, u32[]{:S(2)}, u32[]{:S(2)}) async-start(bf16[64,6,1024]{2,1,0:T(8,128)(2,1)} %reshape.98), calls=%async_computation.3 | async-start | bytes 2097152 | tf_op jit(solution)/shard_map/all_to_all | solution.py:89
Sparse Core Ops, SparseCore 0:
  10.9 133.5 all-gather.3
  186.6 37.5 all-gather.5
  253.6 41.0 reduce-scatter.1
where the time goes:
time: 347 us; the launch traced here: 346 us
  waiting for transfers between devices  201 us (58%)
  matrix products  42.3 us (12%)
  local copies, waits for them, and re-layouts  36.6 us (11%)
  blocking collectives  35.1 us (10%)
  starting transfers between devices  16 us (5%)
  between operations  13.3 us (4%)
    all_gather x1, waiting for transfers between devices, body(): lax.all_gather(w_join, ('mic', 'seq'), axis=0, tiled=True)  59.5 us
    reduce_scatter x1, waiting for transfers between devices, body(): lax.psum_scatter(result.reshape(lax.axis_size('mic') * (seq_count * exp_l...  41.3 us
    all_gather x1, waiting for transfers between devices, body(): arrived = lax.all_gather(landed[None], 'mic', axis=0, tiled=True)  37.7 us
    all_to_all x1, waiting for transfers between devices, body(): lax.all_to_all(projected, 'mic', split_axis=1, concat_axis=0, tiled=True)  35.4 us
    all_to_all x1, blocking collectives, body(): lax.all_to_all(buffers, 'seq', split_axis=0, concat_axis=0, tiled=True)  35.1 us
    all_to_all x1, waiting for transfers between devices, body(): lax.all_to_all(summed, 'seq', split_axis=0, concat_axis=0, tiled=True)  26.5 us
    all_to_all x1, starting transfers between devices, body(): lax.all_to_all(summed, 'seq', split_axis=0, concat_axis=0, tiled=True)  10.8 us
    dot_general x1, matrix products, body(): jnp.einsum('nejf,efd->nejd', inner, w_down, preferred_element_type=jnp.fl...  10.6 us
  transfers between devices with their start and end apart: 5, of which 5 were waited for; matrix products, arithmetic and copies ran while one was open for 11% of the time, Pallas kernels for 0%

commit v1 on v0

--- a/solution.py
+++ b/solution.py
@@ -42,7 +42,12 @@
     attended = mixed_heads.astype(jnp.bfloat16).reshape(frame_count, MICS * chan_width)
     joined = jnp.dot(
         attended,
-        lax.all_gather(w_join, ("mic", "seq"), axis=0, tiled=True),
+        jnp.concatenate(
+            lax.all_to_all(
+                jnp.stack([w_join] * lax.axis_size(("mic", "seq"))), ("mic", "seq"), 0, 0
+            ),
+            axis=0,
+        ),
         preferred_element_type=jnp.float32,
     )
     scale_row = lax.rsqrt(jnp.mean(joined * joined, axis=-1, keepdims=True) + 1e-06)

time: 347 us -> 461 us (1.33)
  waiting for transfers between devices: 201 us -> 261 us
  blocking collectives: 35.1 us -> 75.1 us
  starting transfers between devices: 16 us -> 25.9 us
    all_to_all x1, waiting for transfers between devices: 35.4 us -> 156 us  [body(): lax.all_to_all(jnp.stack([w_join] * lax.axis_size(('mic', 'seq'))), ('mic...]
    all_gather x1 -> x0, waiting for transfers between devices: 59.5 us -> none  [body(): lax.all_gather(w_join, ('mic', 'seq'), axis=0, tiled=True)]
    all_to_all x0 -> x1, blocking collectives: none -> 41.5 us  [body(): lax.all_to_all(projected, 'mic', split_axis=1, concat_axis=0, tiled=True)]
    all_to_all x1, starting transfers between devices: 5.14 us -> 15 us  [body(): lax.all_to_all(jnp.stack([w_join] * lax.axis_size(('mic', 'seq'))), ('mic...]
  transfers between devices with their start and end apart: 5 -> 4, of which waited for: 5 -> 4; matrix products, arithmetic and copies ran while one was open for 11% -> 7% of each run, Pallas kernels for 0% -> 0%
where the time goes in v1:
time: 461 us
  waiting for transfers between devices  261 us (57%)
  blocking collectives  75.1 us (16%)
  matrix products  42.6 us (9%)
  local copies, waits for them, and re-layouts  40 us (9%)
  starting transfers between devices  25.9 us (6%)
  between operations  13.6 us (3%)
    all_to_all x1, waiting for transfers between devices, body(): lax.all_to_all(jnp.stack([w_join] * lax.axis_size(('mic', 'seq'))), ('mic...  156 us
    all_to_all x1, blocking collectives, body(): lax.all_to_all(projected, 'mic', split_axis=1, concat_axis=0, tiled=True)  41.5 us
    reduce_scatter x1, waiting for transfers between devices, body(): lax.psum_scatter(result.reshape(lax.axis_size('mic') * (seq_count * exp_l...  41.3 us
    all_gather x1, waiting for transfers between devices, body(): arrived = lax.all_gather(landed[None], 'mic', axis=0, tiled=True)  37.4 us
    all_to_all x1, blocking collectives, body(): lax.all_to_all(buffers, 'seq', split_axis=0, concat_axis=0, tiled=True)  33.7 us
    all_to_all x1, waiting for transfers between devices, body(): lax.all_to_all(summed, 'seq', split_axis=0, concat_axis=0, tiled=True)  26.5 us
    all_to_all x1, starting transfers between devices, body(): lax.all_to_all(jnp.stack([w_join] * lax.axis_size(('mic', 'seq'))), ('mic...  15 us
    all_to_all x1, starting transfers between devices, body(): lax.all_to_all(summed, 'seq', split_axis=0, concat_axis=0, tiled=True)  10.8 us
  transfers between devices with their start and end apart: 4, of which 4 were waited for; matrix products, arithmetic and copies ran while one was open for 7% of the time, Pallas kernels for 0%

profile of v1, /device:TPU:1, one launch (start us, length us, event | category | flops | bytes accessed | tf_op | source)
XLA Modules:
  0.0 460.7 jit_solution(8314329188484194143)
XLA Ops:
  6.5 1.9 copy-done
  8.4 3.0 convolution_convert_fusion
  11.7 41.5 %all_to_all.30 = bf16[2,4,128,1536]{3,2,0,1:T(8,128)(2,1)S(1)} all-to-all(bf16[2,4,128,1536]{3,2,0,1:T(8,128)(2,1)S(1)} %copy.26), channel_id=1, replica_groups=mesh['mic'=4,'seq'=64] {'mic'}, dimensions={1} | all-to-all | bytes 6291456 | tf_op jit(solution)/shard_map/all_to_all | solution.py:25
  53.1 4.3 stack.4
  57.4 15.0 %all-to-all-start.1 = ((bf16[256,16,1024]{2,1,0:T(8,128)(2,1)}), bf16[256,16,1024]{2,1,0:T(8,128)(2,1)}, u32[]{:S(2)}, u32[]{:S(2)}) async-start(bf16[256,16,1024]{2,1,0:T(8,128)(2,1)} %stack.4), calls=%async_computation.1 | async-start | bytes 16777216 | tf_op jit(solution)/shard_map/all_to_all | solution.py:46
  76.6 3.8 copy.32
  81.1 3.8 copy.30
  85.5 3.8 copy.31
  89.3 7.3 %fusion.38 = (f32[128,8,8]{2,1,0:T(8,128)S(1)}, f32[128,8,8,8]{2,3,1,0:T(8,128)}) fusion(bf16[8,128,8,64]{3,0,2,1:T(8,128)(2,1)} %copy.30, bf16[8,128,8,64]{3,0,2,1:T(8,128)(2,1)} %copy.31), kind=kOutput, calls=%fused_computation.56 | convolution fusion | flops 8585223 | bytes 2392064 | tf_op jit(solution)/shard_map/sub | solution.py:37
  96.6 4.2 convert_bitcast_fusion.1
  100.8 3.2 copy.34
  104.0 156.1 %all-to-all-done.1 = bf16[256,16,1024]{2,1,0:T(8,128)(2,1)} async-done(((bf16[256,16,1024]{2,1,0:T(8,128)(2,1)}), bf16[256,16,1024]{2,1,0:T(8,128)(2,1)}, u32[]{:S(2)}, u32[]{:S(2)}) %all-to-all-start.1) | async-done | bytes 8388640 | tf_op jit(solution)/shard_map/all_to_all | solution.py:46
  260.1 4.7 %multiply_reduce_fusion.1 = (f32[128]{0:T(128)S(1)}, f32[128,1024]{1,0:T(8,128)S(1)}) fusion(bf16[128,4096]{0,1:T(8,128)(2,1)S(1)} %bitcast.103, bf16[4096,1024]{1,0:T(8,128)(2,1)} %bitcast.11), kind=kOutput, calls=%fused_computation.33 | convolution fusion | flops 1074003840 | bytes 9961984 | tf_op jit(solution)/shard_map/dot_general | solution.py:43
  265.6 33.7 %all_to_all.31 = bf16[64,6,1024]{2,1,0:T(8,128)(2,1)S(1)} all-to-all(bf16[64,6,1024]{2,1,0:T(8,128)(2,1)S(1)} %reshape.98), channel_id=1, replica_groups=mesh['mic'=4,'seq'=64] {'seq'}, dimensions={0} | all-to-all | bytes 1572864 | tf_op jit(solution)/shard_map/all_to_all | solution.py:75
  300.7 37.4 %all-gather.3.cloned.1.call-done = bf16[256,6,1024]{2,0,1:T(8,128)(2,1)} async-done(((bf16[64,6,1024]{2,0,1:T(8,128)(2,1)}), bf16[256,6,1024]{2,0,1:T(8,128)(2,1)}) %all-gather.3.cloned.1.call-update) | async-done | bytes 3145744 | tf_op jit(solution)/shard_map/all_gather | solution.py:76
  338.1 8.6 %fusion.19 = f32[256,6,1024]{2,0,1:T(8,128)} fusion(bf16[256,6,1024]{2,0,1:T(8,128)(2,1)} %all-gather.3.cloned.1.call-done, bf16[1,1024,1024]{2,1,0:T(8,128)(2,1)} %param.14), kind=kOutput, calls=%fused_computation.20 | convolution fusion | flops 3221225472 | bytes 11534336 | tf_op jit(solution)/shard_map/nejd,edf->nejf/dot_general | solution.py:79
  346.7 10.6 %convert_bitcast_fusion = bf16[256,1,6,1024]{3,0,2,1:T(8,128)(2,1)S(1)} fusion(f32[256,6,1024]{2,0,1:T(8,128)} %fusion.19, bf16[256,6,1024]{2,0,1:T(8,128)(2,1)} %all-gather.3.cloned.1.call-done, bf16[1,1024,1024]{2,1,0:T(8,128)(2,1)} %param.16, bf16[1,1024,1024]{2,1,0:T(8,128)(2,1)} %param.15), kind=kOutput, calls=%fused_computation.15 | convolution fusion | flops 6453460992 | bytes 16777216 | tf_op jit(solution)/shard_map/nejf,efd->nejd/dot_general | solution.py:84
  357.3 3.7 copy.40
  361.0 6.3 %convert_element_type.71 = bf16[1536,1024]{1,0:T(8,128)(2,1)} reshape(bf16[256,1,6,1024]{3,2,0,1:T(8,128)(2,1)} %copy.40) | data formatting | bytes 6291456 | tf_op jit(solution)/shard_map/convert_element_type | solution.py:88
  367.4 41.3 %reduce-scatter.2.cloned.1.call-done = bf16[384,1024]{1,0:T(8,128)(2,1)} async-done(((bf16[1536,1024]{1,0:T(8,128)(2,1)}), bf16[384,1024]{1,0:T(8,128)(2,1)}) %reduce-scatter.2.cloned.1.call-update) | async-done | bytes 786448 | tf_op jit(solution)/shard_map/reduce_scatter | solution.py:85
  408.6 2.3 reshape.104
  411.0 10.8 %all-to-all-start.3 = ((bf16[64,6,1024]{2,1,0:T(8,128)(2,1)}), bf16[64,6,1024]{2,1,0:T(8,128)(2,1)}, u32[]{:S(2)}, u32[]{:S(2)}) async-start(bf16[64,6,1024]{2,1,0:T(8,128)(2,1)} %reshape.104), calls=%async_computation.4 | async-start | bytes 2097152 | tf_op jit(solution)/shard_map/all_to_all | solution.py:94
  423.2 26.5 %all-to-all-done.3 = bf16[64,6,1024]{2,1,0:T(8,128)(2,1)} async-done(((bf16[64,6,1024]{2,1,0:T(8,128)(2,1)}), bf16[64,6,1024]{2,1,0:T(8,128)(2,1)}, u32[]{:S(2)}, u32[]{:S(2)}) %all-to-all-start.3) | async-done | bytes 786464 | tf_op jit(solution)/shard_map/all_to_all | solution.py:94
  449.7 2.3 fusion.24
  (48 shorter events, 10.9 us)
Async XLA Ops:
  6.5 1.9 copy-start
  11.7 41.5 %copy-start.7 = (bf16[16,1024]{1,0:T(8,128)(2,1)S(1)}, bf16[16,1024]{1,0:T(8,128)(2,1)}, u32[]{:S(2)}) copy-start(bf16[16,1024]{1,0:T(8,128)(2,1)} %param.11) | copy-start | bytes 98308
  57.4 15.1 %copy-start.9 = (s32[1,1,128,2]{2,3,1,0:T(2,128)S(1)}, s32[1,1,128,2]{2,3,1,0:T(2,128)}, u32[]{:S(2)}) copy-start(s32[1,1,128,2]{2,3,1,0:T(2,128)} %param.17) | copy-start | bytes 3076
  57.4 202.7 %all-to-all-start.1 = ((bf16[256,16,1024]{2,1,0:T(8,128)(2,1)}), bf16[256,16,1024]{2,1,0:T(8,128)(2,1)}, u32[]{:S(2)}, u32[]{:S(2)}) async-start(bf16[256,16,1024]{2,1,0:T(8,128)(2,1)} %stack.4), calls=%async_computation.1 | async-start | bytes 16777216 | tf_op jit(solution)/shard_map/all_to_all | solution.py:46
  72.4 265.6 %all-gather.3.cloned.1.call-start = ((), (), s32[]{:S(2)}) async-start(), calls=%async_computation.6 | async-start | bytes 3932160 | tf_op jit(solution)/shard_map/all_gather | solution.py:76
  74.9 5.5 %copy-start.4 = (bf16[8,128,512]{2,1,0:T(8,128)(2,1)S(1)}, bf16[8,128,512]{2,1,0:T(8,128)(2,1)}, u32[]{:S(2)}) copy-start(bf16[8,128,512]{2,1,0:T(8,128)(2,1)} %get-tuple-element.8) | copy-start | bytes 3145732
  80.4 4.4 copy-start.3
  89.3 7.3 %copy-start.5 = (bf16[8,128,8,64]{3,0,2,1:T(8,128)(2,1)S(1)}, bf16[8,128,8,64]{3,0,2,1:T(8,128)(2,1)}, u32[]{:S(2)}) copy-start(bf16[8,128,8,64]{3,0,2,1:T(8,128)(2,1)} %copy.32) | copy-start | bytes 3145732
  260.1 4.8 %copy-start.8 = (f32[1024]{0:T(1024)S(1)}, f32[1024]{0:T(1024)}, u32[]{:S(2)}) copy-start(f32[1024]{0:T(1024)} %param.12) | copy-start | bytes 12292
  264.9 35.7 %copy-start.2 = (f32[128,1024]{1,0:T(8,128)}, f32[128,1024]{1,0:T(8,128)S(1)}, u32[]{:S(2)}) copy-start(f32[128,1024]{1,0:T(8,128)S(1)} %get-tuple-element.13) | copy-start | bytes 1572868
  300.6 108.0 %reduce-scatter.2.cloned.1.call-start = ((), (), s32[]{:S(2)}) async-start(), calls=%async_computation.5 | async-start | bytes 3932160 | tf_op jit(solution)/shard_map/reduce_scatter | solution.py:85
  367.4 54.4 %copy-start.6 = (bf16[1024,64]{0,1:T(8,128)(2,1)S(1)}, bf16[1024,64]{0,1:T(8,128)(2,1)}, u32[]{:S(2)}) copy-start(bf16[1024,64]{0,1:T(8,128)(2,1)} %param.13) | copy-start | bytes 393220
  408.6 45.2 %copy-start.1 = (bf16[2,512,1536]{2,1,0:T(8,128)(2,1)S(1)}, bf16[2,512,1536]{2,1,0:T(8,128)(2,1)}, u32[]{:S(2)}) copy-start(bf16[2,512,1536]{2,1,0:T(8,128)(2,1)} %param.10) | copy-start | bytes 9437188
  411.0 38.7 %all-to-all-start.3 = ((bf16[64,6,1024]{2,1,0:T(8,128)(2,1)}), bf16[64,6,1024]{2,1,0:T(8,128)(2,1)}, u32[]{:S(2)}, u32[]{:S(2)}) async-start(bf16[64,6,1024]{2,1,0:T(8,128)(2,1)} %reshape.104), calls=%async_computation.4 | async-start | bytes 2097152 | tf_op jit(solution)/shard_map/all_to_all | solution.py:94
Sparse Core Ops, SparseCore 0:
  300.7 37.2 all-gather.2
  367.5 41.0 reduce-scatter.1
